TPU v7x, 512 devices: a whole 4x4x16 slice. The times are simulated.
512 devices in a mesh: blk: 64 (over z, x_lo, core), rep: 8 (over y, x_hi).
Axes of the slice: x: 4 (x_hi: 2, x_lo: 2; x = x_hi * 2 + x_lo), y: 4, z: 16, core: 2. Of those that a mesh axis runs over, the one named last changes fastest.
Arguments:
- features: bfloat16 [65536, 256], P(('blk', 'rep')), may hold values from -6 to 6
- out_grad: bfloat16 [65536, 256], P('blk'), may hold values from -4 to 4
- weight: bfloat16 [256, 256], replicated, may hold values from -0.375 to 0.375
- block_words: int32 [64, 64, 8, 16, 128], P('blk', 'rep'), may hold values from 0 to 255
- block_coords: int32 [64, 64, 2, 8], P('blk', 'rep'), may hold values from 0 to 7, as said below
- block_counts: int32 [64, 64], P('blk', 'rep'), may hold values from 1 to 8, as said below
- degrees: int32 [65536], P('blk'), may hold values from 1 to 127
Outputs:
- input_grad: bfloat16 [65536, 256], P(('blk', 'rep'))
- weight_grad: float32 [256, 256], replicated
Inputs may be any that keep to these rules, and one draw needn't show every extreme that they name: `block_coords`: within one slab pair the 8 slots name distinct pairs of row block and column block. `block_counts`: the 8 slab pairs of one device include one in which all 8 slots are live.
All inputs are finite; a program needn't handle non-finite values.
Results may differ from a plain program's by a relative error of at most 0.015.
Values may be sent and summed in bfloat16 or wider, within the bound.
A program may use at most 64 MiB of HBM per device.

v0:
```python
import math
import jax
import jax.numpy as jnp
from jax import lax
from jax.sharding import PartitionSpec as P


def from_behind(block, axis, distance):
    devices = range(lax.axis_size(axis))
    route = [((i - distance) % len(devices), i) for i in devices]
    return lax.ppermute(block, axis, route)


def unpack_block(slot_words):
    shifts = jnp.arange(8, dtype=jnp.int32)
    bit_values = jnp.bitwise_and(
        jnp.right_shift(slot_words[:, :, None, :], shifts[None, None, :, None]), 1
    )
    return bit_values.reshape(slot_words.shape[0], 128, 128).astype(jnp.bfloat16)


def per_device(features, out_grad, weight, block_words, block_coords, block_counts, degrees):
    slab_rows, width = out_grad.shape
    row_blocks = slab_rows // 128
    group_size = lax.axis_size("rep")
    step_count = lax.axis_size("blk") // group_size
    rep_index = lax.axis_index("rep")
    inverse_root = lax.rsqrt(degrees.astype(jnp.float32))
    scaled = (out_grad.astype(jnp.float32) * inverse_root[:, None]).astype(jnp.bfloat16)
    column_ids = jnp.arange(row_blocks, dtype=jnp.int32)
    slot_total = block_words.shape[2]
    slot_ids = jnp.arange(slot_total, dtype=jnp.int32)

    def add_slot(accumulated, source_slab, slot_index):
        slot_words = lax.dynamic_index_in_dim(block_words[0], slot_index, 0, keepdims=False)
        coords = lax.dynamic_index_in_dim(block_coords[0], slot_index, 0, keepdims=False)
        live_count = lax.dynamic_index_in_dim(block_counts[0], slot_index, 0, keepdims=False)
        picked = jnp.take(source_slab.reshape(row_blocks, 128, width), coords[0], axis=0)
        transposed = unpack_block(slot_words)
        contrib = jnp.einsum("bvu,buf->bvf", transposed, picked, preferred_element_type=jnp.float32)
        live_slots = slot_ids < live_count
        placement = ((coords[1][:, None] == column_ids[None, :]) & live_slots[:, None]).astype(
            jnp.float32
        )
        return accumulated + jnp.einsum("bc,bvf->cvf", placement, contrib)

    empty = jnp.zeros((row_blocks, 128, width), jnp.float32)
    current = scaled
    for bit in range(group_size.bit_length() - 1):
        shifted = from_behind(current, "blk", -(1 << bit) * step_count)
        current = jnp.where(
            jnp.bitwise_and(jnp.right_shift(rep_index, bit), 1) == 1, shifted, current
        )
    accumulated = add_slot(empty, current, 0)

    def advance(step_index, state_tuple):
        current, accumulated = state_tuple
        current = from_behind(current, "blk", -1)
        return (current, add_slot(accumulated, current, step_index))

    current, accumulated = lax.fori_loop(1, step_count, advance, (current, accumulated))
    partial_sums = accumulated.reshape(slab_rows, width)
    share_rows = slab_rows // group_size
    share_root = lax.dynamic_slice_in_dim(inverse_root, rep_index * share_rows, share_rows, 0)
    whole_sums = lax.psum(partial_sums, "rep")
    own_sums = lax.dynamic_slice_in_dim(whole_sums, rep_index * share_rows, share_rows, 0)
    aggregated = (own_sums * share_root[:, None]).astype(jnp.bfloat16)
    input_grad = lax.dot_general(
        aggregated, weight, (((1,), (1,)), ((), ())), preferred_element_type=jnp.float32
    ).astype(jnp.bfloat16)
    weight_term = lax.dot_general(
        features, aggregated, (((0,), (0,)), ((), ())), preferred_element_type=jnp.float32
    )
    node_total = slab_rows * lax.axis_size("blk")
    weight_grad = lax.psum(weight_term, ("blk", "rep")) * (1.0 / math.sqrt(node_total))
    return (input_grad, weight_grad)


def solution(mesh):
    return jax.shard_map(
        per_device,
        mesh=mesh,
        in_specs=(
            P(("blk", "rep"), None),
            P("blk", None),
            P(),
            P("blk", "rep", None, None, None),
            P("blk", "rep", None, None),
            P("blk", "rep"),
            P("blk"),
        ),
        out_specs=(P(("blk", "rep"), None), P()),
        check_vma=False,
    )
```

profile of v0, /device:TPU:4, one launch (start us, length us, event | category | flops | bytes accessed | tf_op | source)
XLA Modules:
  0.0 821.2 jit_solution(11861567313591803345)
XLA Ops:
  9.3 11.8 %collective-permute-start.1 = (bf16[1024,256]{1,0:T(8,128)(2,1)S(1)}, bf16[1024,256]{1,0:T(8,128)(2,1)S(1)}, u32[]{:S(2)}, u32[]{:S(2)}) collective-permute-start(bf16[1024,256]{1,0:T(8,128)(2,1)S(1)} %multiply_convert_fusion), channel_id=1, source_target_pairs={{64,0},{72,8},{80,16},{88,24},{96,32},{104,40},{112,48},{120,56},{... | collective-permute-start | bytes 1572872 | tf_op jit(solution)/shard_map/ppermute | solution.py:11
  21.1 22.4 %collective-permute-done.1 = bf16[1024,256]{1,0:T(8,128)(2,1)S(1)} collective-permute-done((bf16[1024,256]{1,0:T(8,128)(2,1)S(1)}, bf16[1024,256]{1,0:T(8,128)(2,1)S(1)}, u32[]{:S(2)}, u32[]{:S(2)}) %collective-permute-start.1) | collective-permute-done | bytes 524320 | tf_op jit(solution)/shard_map/ppermute | solution.py:11
  43.8 6.3 collective-permute-start.2
  51.0 40.0 %collective-permute-done.2 = bf16[1024,256]{1,0:T(8,128)(2,1)S(1)} collective-permute-done((bf16[1024,256]{1,0:T(8,128)(2,1)S(1)}, bf16[1024,256]{1,0:T(8,128)(2,1)S(1)}, u32[]{:S(2)}, u32[]{:S(2)}) %collective-permute-start.2) | collective-permute-done | bytes 524320 | tf_op jit(solution)/shard_map/ppermute | solution.py:11
  91.1 5.0 collective-permute-start.3
  98.3 28.4 %collective-permute-done.3 = bf16[1024,256]{1,0:T(8,128)(2,1)S(1)} collective-permute-done((bf16[1024,256]{1,0:T(8,128)(2,1)S(1)}, bf16[1024,256]{1,0:T(8,128)(2,1)S(1)}, u32[]{:S(2)}, u32[]{:S(2)}) %collective-permute-start.3) | collective-permute-done | bytes 524320 | tf_op jit(solution)/shard_map/ppermute | solution.py:11
  128.1 121.5 %while.20 = (s32[]{:T(128)}, bf16[1024,256]{1,0:T(8,128)(2,1)S(1)}, f32[8,128,256]{2,0,1:T(8,128)S(1)}, s32[1,8,2,8]{3,2,1,0:T(2,128)}, s32[1,8]{1,0:T(1,128)S(1...) while((s32[]{:T(128)}, bf16[1024,256]{1,0:T(8,128)(2,1)S(1)}, ...), condition=%wide.region_1.3_spmd.clone.clone, body=%wide.region_0.2_spmd.clone.clone.sunk | while | flops 72221880 | bytes 8067647 | solution.py:61
  128.2 29.0 %collective-permute-start = (bf16[1024,256]{1,0:T(8,128)(2,1)S(1)}, bf16[1024,256]{1,0:T(8,128)(2,1)S(1)}, u32[]{:S(2)}, u32[]{:S(2)}) collective-permute-start(bf16[1024,256]{1,0:T(8,128)(2,1)S(1)} %get-tuple-element.308), channel_id=1, source_target_pairs={{8,0},{16,8},{24,16},{32,24},{40,32},{48,40},{56,48},{64,56},{72,6... | collective-permute-start | bytes 1572872 | tf_op jit(solution)/shard_map/while/body/eval_jaxpr/ppermute | solution.py:11
  160.1 3.8 collective-permute-done
  165.3 5.9 collective-permute-start
  174.2 3.8 collective-permute-done
  179.4 5.9 collective-permute-start
  188.2 3.8 collective-permute-done
  193.4 5.9 collective-permute-start
  202.3 3.8 collective-permute-done
  207.5 5.9 collective-permute-start
  216.3 3.8 collective-permute-done
  221.6 5.9 collective-permute-start
  230.4 3.8 collective-permute-done
  235.6 5.9 collective-permute-start
  244.5 3.8 collective-permute-done
  251.2 97.1 %all-reduce.3.cloned.1.call-done = f32[1024,256]{1,0:T(8,128)} async-done(((f32[1024,256]{1,0:T(8,128)}), f32[1024,256]{1,0:T(8,128)}) %all-reduce.3.cloned.1.call-update) | async-done | bytes 1048592 | tf_op jit(solution)/shard_map/psum | solution.py:65
  348.3 1.9 convolution_bitcast_fusion
  352.0 460.6 %all-reduce.5.cloned.1.call-done = f32[256,256]{0,1:T(8,128)} async-done(((f32[256,256]{0,1:T(8,128)}), f32[256,256]{0,1:T(8,128)}) %all-reduce.5.cloned.1.call-update) | async-done | bytes 262160 | tf_op jit(solution)/shard_map/psum | solution.py:75
  (123 shorter events, 41.9 us)
Async XLA Ops:
  7.2 343.1 %copy-start = (bf16[256,256]{1,0:T(8,128)(2,1)S(1)}, bf16[256,256]{1,0:T(8,128)(2,1)}, u32[]{:S(2)}) copy-start(bf16[256,256]{1,0:T(8,128)(2,1)} %param.13) | copy-start | bytes 393220
  7.2 341.1 %all-reduce.3.cloned.1.call-start = ((), (), s32[]{:S(2)}) async-start(), calls=%async_computation | async-start | bytes 2097152 | tf_op jit(solution)/shard_map/psum | solution.py:65
  7.9 35.6 %copy-start.1 = (bf16[1024,256]{1,0:T(8,128)(2,1)S(1)}, bf16[1024,256]{1,0:T(8,128)(2,1)}, u32[]{:S(2)}) copy-start(bf16[1024,256]{1,0:T(8,128)(2,1)} %param.12) | copy-start | bytes 1572868
  9.3 34.2 %collective-permute-start.1 = (bf16[1024,256]{1,0:T(8,128)(2,1)S(1)}, bf16[1024,256]{1,0:T(8,128)(2,1)S(1)}, u32[]{:S(2)}, u32[]{:S(2)}) collective-permute-start(bf16[1024,256]{1,0:T(8,128)(2,1)S(1)} %multiply_convert_fusion), channel_id=1, source_target_pairs={{64,0},{72,8},{80,16},{88,24},{96,32},{104,40},{112,48},{120,56},{... | collective-permute-start | bytes 1572872 | tf_op jit(solution)/shard_map/ppermute | solution.py:11
  43.8 47.2 %collective-permute-start.2 = (bf16[1024,256]{1,0:T(8,128)(2,1)S(1)}, bf16[1024,256]{1,0:T(8,128)(2,1)S(1)}, u32[]{:S(2)}, u32[]{:S(2)}) collective-permute-start(bf16[1024,256]{1,0:T(8,128)(2,1)S(1)} %broadcast_select_fusion), channel_id=1, source_target_pairs={{128,0},{136,8},{144,16},{152,24},{160,32},{168,40},{176,48},{184,... | collective-permute-start | bytes 1572872 | tf_op jit(solution)/shard_map/ppermute | solution.py:11
  91.1 35.7 %collective-permute-start.3 = (bf16[1024,256]{1,0:T(8,128)(2,1)S(1)}, bf16[1024,256]{1,0:T(8,128)(2,1)S(1)}, u32[]{:S(2)}, u32[]{:S(2)}) collective-permute-start(bf16[1024,256]{1,0:T(8,128)(2,1)S(1)} %broadcast_select_fusion.1), channel_id=1, source_target_pairs={{256,0},{264,8},{272,16},{280,24},{288,32},{296,40},{304,48},{312,... | collective-permute-start | bytes 1572872 | tf_op jit(solution)/shard_map/ppermute | solution.py:11
  96.0 0.7 copy-start.3
  128.2 35.7 %collective-permute-start = (bf16[1024,256]{1,0:T(8,128)(2,1)S(1)}, bf16[1024,256]{1,0:T(8,128)(2,1)S(1)}, u32[]{:S(2)}, u32[]{:S(2)}) collective-permute-start(bf16[1024,256]{1,0:T(8,128)(2,1)S(1)} %get-tuple-element.308), channel_id=1, source_target_pairs={{8,0},{16,8},{24,16},{32,24},{40,32},{48,40},{56,48},{64,56},{72,6... | collective-permute-start | bytes 1572872 | tf_op jit(solution)/shard_map/while/body/eval_jaxpr/ppermute | solution.py:11
  165.3 12.6 %collective-permute-start = (bf16[1024,256]{1,0:T(8,128)(2,1)S(1)}, bf16[1024,256]{1,0:T(8,128)(2,1)S(1)}, u32[]{:S(2)}, u32[]{:S(2)}) collective-permute-start(bf16[1024,256]{1,0:T(8,128)(2,1)S(1)} %get-tuple-element.308), channel_id=1, source_target_pairs={{8,0},{16,8},{24,16},{32,24},{40,32},{48,40},{56,48},{64,56},{72,6... | collective-permute-start | bytes 1572872 | tf_op jit(solution)/shard_map/while/body/eval_jaxpr/ppermute | solution.py:11
  179.4 12.6 %collective-permute-start = (bf16[1024,256]{1,0:T(8,128)(2,1)S(1)}, bf16[1024,256]{1,0:T(8,128)(2,1)S(1)}, u32[]{:S(2)}, u32[]{:S(2)}) collective-permute-start(bf16[1024,256]{1,0:T(8,128)(2,1)S(1)} %get-tuple-element.308), channel_id=1, source_target_pairs={{8,0},{16,8},{24,16},{32,24},{40,32},{48,40},{56,48},{64,56},{72,6... | collective-permute-start | bytes 1572872 | tf_op jit(solution)/shard_map/while/body/eval_jaxpr/ppermute | solution.py:11
  193.4 12.6 %collective-permute-start = (bf16[1024,256]{1,0:T(8,128)(2,1)S(1)}, bf16[1024,256]{1,0:T(8,128)(2,1)S(1)}, u32[]{:S(2)}, u32[]{:S(2)}) collective-permute-start(bf16[1024,256]{1,0:T(8,128)(2,1)S(1)} %get-tuple-element.308), channel_id=1, source_target_pairs={{8,0},{16,8},{24,16},{32,24},{40,32},{48,40},{56,48},{64,56},{72,6... | collective-permute-start | bytes 1572872 | tf_op jit(solution)/shard_map/while/body/eval_jaxpr/ppermute | solution.py:11
  207.5 12.6 %collective-permute-start = (bf16[1024,256]{1,0:T(8,128)(2,1)S(1)}, bf16[1024,256]{1,0:T(8,128)(2,1)S(1)}, u32[]{:S(2)}, u32[]{:S(2)}) collective-permute-start(bf16[1024,256]{1,0:T(8,128)(2,1)S(1)} %get-tuple-element.308), channel_id=1, source_target_pairs={{8,0},{16,8},{24,16},{32,24},{40,32},{48,40},{56,48},{64,56},{72,6... | collective-permute-start | bytes 1572872 | tf_op jit(solution)/shard_map/while/body/eval_jaxpr/ppermute | solution.py:11
  221.6 12.6 %collective-permute-start = (bf16[1024,256]{1,0:T(8,128)(2,1)S(1)}, bf16[1024,256]{1,0:T(8,128)(2,1)S(1)}, u32[]{:S(2)}, u32[]{:S(2)}) collective-permute-start(bf16[1024,256]{1,0:T(8,128)(2,1)S(1)} %get-tuple-element.308), channel_id=1, source_target_pairs={{8,0},{16,8},{24,16},{32,24},{40,32},{48,40},{56,48},{64,56},{72,6... | collective-permute-start | bytes 1572872 | tf_op jit(solution)/shard_map/while/body/eval_jaxpr/ppermute | solution.py:11
  235.6 12.6 %collective-permute-start = (bf16[1024,256]{1,0:T(8,128)(2,1)S(1)}, bf16[1024,256]{1,0:T(8,128)(2,1)S(1)}, u32[]{:S(2)}, u32[]{:S(2)}) collective-permute-start(bf16[1024,256]{1,0:T(8,128)(2,1)S(1)} %get-tuple-element.308), channel_id=1, source_target_pairs={{8,0},{16,8},{24,16},{32,24},{40,32},{48,40},{56,48},{64,56},{72,6... | collective-permute-start | bytes 1572872 | tf_op jit(solution)/shard_map/while/body/eval_jaxpr/ppermute | solution.py:11
  251.0 97.3 %copy-start.2 = (bf16[128,256]{1,0:T(8,128)(2,1)S(1)}, bf16[128,256]{1,0:T(8,128)(2,1)}, u32[]{:S(2)}) copy-start(bf16[128,256]{1,0:T(8,128)(2,1)} %param.11) | copy-start | bytes 196612
  251.0 561.5 %all-reduce.5.cloned.1.call-start = ((), (), s32[]{:S(2)}) async-start(), calls=%async_computation.1 | async-start | bytes 524288 | tf_op jit(solution)/shard_map/psum | solution.py:75
Sparse Core Ops, SparseCore 0:
  251.2 97.1 all-reduce.2
  354.3 458.2 all-reduce.4
where the time goes:
time: 822 us; the launch traced here: 821 us
  waiting for transfers between devices  675 us (82%)
  starting transfers between devices  87.8 us (11%)
  local copies, waits for them, and re-layouts  24.9 us (3%)
  between operations  14.2 us (2%)
  matrix products  9.97 us (1%)
  other arithmetic  8.83 us (1%)
    psum x1, waiting for transfers between devices, per_device(): lax.psum(weight_term, ('blk', 'rep')) * (1.0 / math.sqrt(node_total))  461 us
    ppermute x10, waiting for transfers between devices, from_behind(): return lax.ppermute(block, axis, route)  117 us
    psum x1, waiting for transfers between devices, per_device(): whole_sums = lax.psum(partial_sums, 'rep')  97.1 us
    ppermute x10, starting transfers between devices, from_behind(): return lax.ppermute(block, axis, route)  87.7 us
  transfers between devices with their start and end apart: 12, of which 12 were waited for; matrix products, arithmetic and copies ran while one was open for 3% of the time, Pallas kernels for 0%

commit v1 on v0

--- a/solution.py
+++ b/solution.py
@@ -72,7 +72,7 @@
         features, aggregated, (((0,), (0,)), ((), ())), preferred_element_type=jnp.float32
     )
     node_total = slab_rows * lax.axis_size("blk")
-    weight_grad = lax.psum(weight_term, ("blk", "rep")) * (1.0 / math.sqrt(node_total))
+    weight_grad = lax.psum(lax.psum(weight_term, "rep"), "blk") * (1.0 / math.sqrt(node_total))
     return (input_grad, weight_grad)
 
 

time: 822 us -> 867 us (1.055)
  the two profiles are of different devices: /device:TPU:4 before, /device:TPU:1 now
where the time goes in v1:
time: 867 us; the launch traced here: 866 us
  waiting for transfers between devices  704 us (81%)
  starting transfers between devices  104 us (12%)
  local copies, waits for them, and re-layouts  24.9 us (3%)
  between operations  13.9 us (2%)
  matrix products  9.98 us (1%)
  other arithmetic  8.83 us (1%)
    psum x1, waiting for transfers between devices, per_device(): lax.psum(lax.psum(weight_term, 'rep'), 'blk')  408 us
    ppermute x10, starting transfers between devices, from_behind(): return lax.ppermute(block, axis, route)  104 us
    psum x1, waiting for transfers between devices, per_device(): whole_sums = lax.psum(partial_sums, 'rep')  102 us
    psum x1, waiting for transfers between devices, per_device(): lax.psum(weight_term, 'rep')  99 us
    ppermute x10, waiting for transfers between devices, from_behind(): return lax.ppermute(block, axis, route)  95.1 us
  transfers between devices with their start and end apart: 13, of which 7 were waited for; matrix products, arithmetic and copies ran while one was open for 3% of the time, Pallas kernels for 0%

profile of v1, /device:TPU:1, one launch (start us, length us, event | category | flops | bytes accessed | tf_op | source)
XLA Modules:
  0.0 866.4 jit_solution(16859872240645736585)
XLA Ops:
  7.9 1.3 multiply_convert_fusion
  9.3 12.4 %collective-permute-start.1 = (bf16[1024,256]{1,0:T(8,128)(2,1)S(1)}, bf16[1024,256]{1,0:T(8,128)(2,1)S(1)}, u32[]{:S(2)}, u32[]{:S(2)}) collective-permute-start(bf16[1024,256]{1,0:T(8,128)(2,1)S(1)} %multiply_convert_fusion), channel_id=1, source_target_pairs={{64,0},{72,8},{80,16},{88,24},{96,32},{104,40},{112,48},{120,56},{... | collective-permute-start | bytes 1572872 | tf_op jit(solution)/shard_map/ppermute | solution.py:11
  21.7 21.9 %collective-permute-done.1 = bf16[1024,256]{1,0:T(8,128)(2,1)S(1)} collective-permute-done((bf16[1024,256]{1,0:T(8,128)(2,1)S(1)}, bf16[1024,256]{1,0:T(8,128)(2,1)S(1)}, u32[]{:S(2)}, u32[]{:S(2)}) %collective-permute-start.1) | collective-permute-done | bytes 524320 | tf_op jit(solution)/shard_map/ppermute | solution.py:11
  43.9 6.5 collective-permute-start.2
  51.2 40.6 %collective-permute-done.2 = bf16[1024,256]{1,0:T(8,128)(2,1)S(1)} collective-permute-done((bf16[1024,256]{1,0:T(8,128)(2,1)S(1)}, bf16[1024,256]{1,0:T(8,128)(2,1)S(1)}, u32[]{:S(2)}, u32[]{:S(2)}) %collective-permute-start.2) | collective-permute-done | bytes 524320 | tf_op jit(solution)/shard_map/ppermute | solution.py:11
  91.9 4.8 collective-permute-start.3
  98.9 27.5 %collective-permute-done.3 = bf16[1024,256]{1,0:T(8,128)(2,1)S(1)} collective-permute-done((bf16[1024,256]{1,0:T(8,128)(2,1)S(1)}, bf16[1024,256]{1,0:T(8,128)(2,1)S(1)}, u32[]{:S(2)}, u32[]{:S(2)}) %collective-permute-start.3) | collective-permute-done | bytes 524320 | tf_op jit(solution)/shard_map/ppermute | solution.py:11
  127.8 115.9 %while.20 = (s32[]{:T(128)}, bf16[1024,256]{1,0:T(8,128)(2,1)S(1)}, f32[8,128,256]{2,0,1:T(8,128)S(1)}, s32[1,8,2,8]{3,2,1,0:T(2,128)}, s32[1,8]{1,0:T(1,128)S(1...) while((s32[]{:T(128)}, bf16[1024,256]{1,0:T(8,128)(2,1)S(1)}, ...), condition=%wide.region_1.3_spmd.clone.clone, body=%wide.region_0.2_spmd.clone.clone.sunk | while | flops 72221880 | bytes 8067647 | solution.py:61
  127.8 3.7 collective-permute-start
  134.5 5.0 collective-permute-done
  141.0 28.1 %collective-permute-start = (bf16[1024,256]{1,0:T(8,128)(2,1)S(1)}, bf16[1024,256]{1,0:T(8,128)(2,1)S(1)}, u32[]{:S(2)}, u32[]{:S(2)}) collective-permute-start(bf16[1024,256]{1,0:T(8,128)(2,1)S(1)} %get-tuple-element.308), channel_id=1, source_target_pairs={{8,0},{16,8},{24,16},{32,24},{40,32},{48,40},{56,48},{64,56},{72,6... | collective-permute-start | bytes 1572872 | tf_op jit(solution)/shard_map/while/body/eval_jaxpr/ppermute | solution.py:11
  173.4 9.7 %collective-permute-start = (bf16[1024,256]{1,0:T(8,128)(2,1)S(1)}, bf16[1024,256]{1,0:T(8,128)(2,1)S(1)}, u32[]{:S(2)}, u32[]{:S(2)}) collective-permute-start(bf16[1024,256]{1,0:T(8,128)(2,1)S(1)} %get-tuple-element.308), channel_id=1, source_target_pairs={{8,0},{16,8},{24,16},{32,24},{40,32},{48,40},{56,48},{64,56},{72,6... | collective-permute-start | bytes 1572872 | tf_op jit(solution)/shard_map/while/body/eval_jaxpr/ppermute | solution.py:11
  187.4 9.7 %collective-permute-start = (bf16[1024,256]{1,0:T(8,128)(2,1)S(1)}, bf16[1024,256]{1,0:T(8,128)(2,1)S(1)}, u32[]{:S(2)}, u32[]{:S(2)}) collective-permute-start(bf16[1024,256]{1,0:T(8,128)(2,1)S(1)} %get-tuple-element.308), channel_id=1, source_target_pairs={{8,0},{16,8},{24,16},{32,24},{40,32},{48,40},{56,48},{64,56},{72,6... | collective-permute-start | bytes 1572872 | tf_op jit(solution)/shard_map/while/body/eval_jaxpr/ppermute | solution.py:11
  201.5 9.7 %collective-permute-start = (bf16[1024,256]{1,0:T(8,128)(2,1)S(1)}, bf16[1024,256]{1,0:T(8,128)(2,1)S(1)}, u32[]{:S(2)}, u32[]{:S(2)}) collective-permute-start(bf16[1024,256]{1,0:T(8,128)(2,1)S(1)} %get-tuple-element.308), channel_id=1, source_target_pairs={{8,0},{16,8},{24,16},{32,24},{40,32},{48,40},{56,48},{64,56},{72,6... | collective-permute-start | bytes 1572872 | tf_op jit(solution)/shard_map/while/body/eval_jaxpr/ppermute | solution.py:11
  215.6 9.7 %collective-permute-start = (bf16[1024,256]{1,0:T(8,128)(2,1)S(1)}, bf16[1024,256]{1,0:T(8,128)(2,1)S(1)}, u32[]{:S(2)}, u32[]{:S(2)}) collective-permute-start(bf16[1024,256]{1,0:T(8,128)(2,1)S(1)} %get-tuple-element.308), channel_id=1, source_target_pairs={{8,0},{16,8},{24,16},{32,24},{40,32},{48,40},{56,48},{64,56},{72,6... | collective-permute-start | bytes 1572872 | tf_op jit(solution)/shard_map/while/body/eval_jaxpr/ppermute | solution.py:11
  229.6 9.7 %collective-permute-start = (bf16[1024,256]{1,0:T(8,128)(2,1)S(1)}, bf16[1024,256]{1,0:T(8,128)(2,1)S(1)}, u32[]{:S(2)}, u32[]{:S(2)}) collective-permute-start(bf16[1024,256]{1,0:T(8,128)(2,1)S(1)} %get-tuple-element.308), channel_id=1, source_target_pairs={{8,0},{16,8},{24,16},{32,24},{40,32},{48,40},{56,48},{64,56},{72,6... | collective-permute-start | bytes 1572872 | tf_op jit(solution)/shard_map/while/body/eval_jaxpr/ppermute | solution.py:11
  241.4 0.9 dynamic-slice_bitcast_fusion.2
  243.7 1.3 copy.10
  245.2 101.7 %all-reduce.4.cloned.1.call-done = f32[1024,256]{1,0:T(8,128)} async-done(((f32[1024,256]{1,0:T(8,128)}), f32[1024,256]{1,0:T(8,128)}) %all-reduce.4.cloned.1.call-update) | async-done | bytes 1048592 | tf_op jit(solution)/shard_map/psum | solution.py:65
  346.9 1.9 convolution_bitcast_fusion
  348.9 99.0 %all-reduce.6.cloned.1.call-done = f32[256,256]{0,1:T(8,128)} async-done(((f32[256,256]{0,1:T(8,128)}), f32[256,256]{0,1:T(8,128)}) %all-reduce.6.cloned.1.call-update) | async-done | bytes 262160 | tf_op jit(solution)/shard_map/psum | solution.py:75
  447.9 1.8 convolution_convert_fusion
  449.7 408.3 %all-reduce.8.cloned.1.call-done = f32[256,256]{0,1:T(8,128)} async-done(((f32[256,256]{0,1:T(8,128)}), f32[256,256]{0,1:T(8,128)}) %all-reduce.8.cloned.1.call-update) | async-done | bytes 262160 | tf_op jit(solution)/shard_map/psum | solution.py:75
  858.0 1.0 broadcast_multiply_fusion
  (126 shorter events, 35.8 us)
Async XLA Ops:
  7.2 440.8 %copy-start = (bf16[256,256]{1,0:T(8,128)(2,1)S(1)}, bf16[256,256]{1,0:T(8,128)(2,1)}, u32[]{:S(2)}) copy-start(bf16[256,256]{1,0:T(8,128)(2,1)} %param.13) | copy-start | bytes 393220
  7.2 339.7 %all-reduce.4.cloned.1.call-start = ((), (), s32[]{:S(2)}) async-start(), calls=%async_computation | async-start | bytes 2097152 | tf_op jit(solution)/shard_map/psum | solution.py:65
  7.9 35.6 %copy-start.1 = (bf16[1024,256]{1,0:T(8,128)(2,1)S(1)}, bf16[1024,256]{1,0:T(8,128)(2,1)}, u32[]{:S(2)}) copy-start(bf16[1024,256]{1,0:T(8,128)(2,1)} %param.12) | copy-start | bytes 1572868
  9.3 34.3 %collective-permute-start.1 = (bf16[1024,256]{1,0:T(8,128)(2,1)S(1)}, bf16[1024,256]{1,0:T(8,128)(2,1)S(1)}, u32[]{:S(2)}, u32[]{:S(2)}) collective-permute-start(bf16[1024,256]{1,0:T(8,128)(2,1)S(1)} %multiply_convert_fusion), channel_id=1, source_target_pairs={{64,0},{72,8},{80,16},{88,24},{96,32},{104,40},{112,48},{120,56},{... | collective-permute-start | bytes 1572872 | tf_op jit(solution)/shard_map/ppermute | solution.py:11
  43.9 48.0 %collective-permute-start.2 = (bf16[1024,256]{1,0:T(8,128)(2,1)S(1)}, bf16[1024,256]{1,0:T(8,128)(2,1)S(1)}, u32[]{:S(2)}, u32[]{:S(2)}) collective-permute-start(bf16[1024,256]{1,0:T(8,128)(2,1)S(1)} %broadcast_select_fusion), channel_id=1, source_target_pairs={{128,0},{136,8},{144,16},{152,24},{160,32},{168,40},{176,48},{184,... | collective-permute-start | bytes 1572872 | tf_op jit(solution)/shard_map/ppermute | solution.py:11
  91.9 34.5 %collective-permute-start.3 = (bf16[1024,256]{1,0:T(8,128)(2,1)S(1)}, bf16[1024,256]{1,0:T(8,128)(2,1)S(1)}, u32[]{:S(2)}, u32[]{:S(2)}) collective-permute-start(bf16[1024,256]{1,0:T(8,128)(2,1)S(1)} %broadcast_select_fusion.1), channel_id=1, source_target_pairs={{256,0},{264,8},{272,16},{280,24},{288,32},{296,40},{304,48},{312,... | collective-permute-start | bytes 1572872 | tf_op jit(solution)/shard_map/ppermute | solution.py:11
  96.6 0.7 copy-start.3
  127.8 11.7 %collective-permute-start = (bf16[1024,256]{1,0:T(8,128)(2,1)S(1)}, bf16[1024,256]{1,0:T(8,128)(2,1)S(1)}, u32[]{:S(2)}, u32[]{:S(2)}) collective-permute-start(bf16[1024,256]{1,0:T(8,128)(2,1)S(1)} %get-tuple-element.308), channel_id=1, source_target_pairs={{8,0},{16,8},{24,16},{32,24},{40,32},{48,40},{56,48},{64,56},{72,6... | collective-permute-start | bytes 1572872 | tf_op jit(solution)/shard_map/while/body/eval_jaxpr/ppermute | solution.py:11
  141.0 31.0 %collective-permute-start = (bf16[1024,256]{1,0:T(8,128)(2,1)S(1)}, bf16[1024,256]{1,0:T(8,128)(2,1)S(1)}, u32[]{:S(2)}, u32[]{:S(2)}) collective-permute-start(bf16[1024,256]{1,0:T(8,128)(2,1)S(1)} %get-tuple-element.308), channel_id=1, source_target_pairs={{8,0},{16,8},{24,16},{32,24},{40,32},{48,40},{56,48},{64,56},{72,6... | collective-permute-start | bytes 1572872 | tf_op jit(solution)/shard_map/while/body/eval_jaxpr/ppermute | solution.py:11
  173.4 12.6 %collective-permute-start = (bf16[1024,256]{1,0:T(8,128)(2,1)S(1)}, bf16[1024,256]{1,0:T(8,128)(2,1)S(1)}, u32[]{:S(2)}, u32[]{:S(2)}) collective-permute-start(bf16[1024,256]{1,0:T(8,128)(2,1)S(1)} %get-tuple-element.308), channel_id=1, source_target_pairs={{8,0},{16,8},{24,16},{32,24},{40,32},{48,40},{56,48},{64,56},{72,6... | collective-permute-start | bytes 1572872 | tf_op jit(solution)/shard_map/while/body/eval_jaxpr/ppermute | solution.py:11
  187.4 12.6 %collective-permute-start = (bf16[1024,256]{1,0:T(8,128)(2,1)S(1)}, bf16[1024,256]{1,0:T(8,128)(2,1)S(1)}, u32[]{:S(2)}, u32[]{:S(2)}) collective-permute-start(bf16[1024,256]{1,0:T(8,128)(2,1)S(1)} %get-tuple-element.308), channel_id=1, source_target_pairs={{8,0},{16,8},{24,16},{32,24},{40,32},{48,40},{56,48},{64,56},{72,6... | collective-permute-start | bytes 1572872 | tf_op jit(solution)/shard_map/while/body/eval_jaxpr/ppermute | solution.py:11
  201.5 12.6 %collective-permute-start = (bf16[1024,256]{1,0:T(8,128)(2,1)S(1)}, bf16[1024,256]{1,0:T(8,128)(2,1)S(1)}, u32[]{:S(2)}, u32[]{:S(2)}) collective-permute-start(bf16[1024,256]{1,0:T(8,128)(2,1)S(1)} %get-tuple-element.308), channel_id=1, source_target_pairs={{8,0},{16,8},{24,16},{32,24},{40,32},{48,40},{56,48},{64,56},{72,6... | collective-permute-start | bytes 1572872 | tf_op jit(solution)/shard_map/while/body/eval_jaxpr/ppermute | solution.py:11
  215.6 12.6 %collective-permute-start = (bf16[1024,256]{1,0:T(8,128)(2,1)S(1)}, bf16[1024,256]{1,0:T(8,128)(2,1)S(1)}, u32[]{:S(2)}, u32[]{:S(2)}) collective-permute-start(bf16[1024,256]{1,0:T(8,128)(2,1)S(1)} %get-tuple-element.308), channel_id=1, source_target_pairs={{8,0},{16,8},{24,16},{32,24},{40,32},{48,40},{56,48},{64,56},{72,6... | collective-permute-start | bytes 1572872 | tf_op jit(solution)/shard_map/while/body/eval_jaxpr/ppermute | solution.py:11
  229.6 12.6 %collective-permute-start = (bf16[1024,256]{1,0:T(8,128)(2,1)S(1)}, bf16[1024,256]{1,0:T(8,128)(2,1)S(1)}, u32[]{:S(2)}, u32[]{:S(2)}) collective-permute-start(bf16[1024,256]{1,0:T(8,128)(2,1)S(1)} %get-tuple-element.308), channel_id=1, source_target_pairs={{8,0},{16,8},{24,16},{32,24},{40,32},{48,40},{56,48},{64,56},{72,6... | collective-permute-start | bytes 1572872 | tf_op jit(solution)/shard_map/while/body/eval_jaxpr/ppermute | solution.py:11
  245.0 101.9 %copy-start.2 = (bf16[128,256]{1,0:T(8,128)(2,1)S(1)}, bf16[128,256]{1,0:T(8,128)(2,1)}, u32[]{:S(2)}) copy-start(bf16[128,256]{1,0:T(8,128)(2,1)} %param.11) | copy-start | bytes 196612
  245.1 202.8 %all-reduce.6.cloned.1.call-start = ((), (), s32[]{:S(2)}) async-start(), calls=%async_computation.1 | async-start | bytes 524288 | tf_op jit(solution)/shard_map/psum | solution.py:75
  348.8 509.2 %all-reduce.8.cloned.1.call-start = ((), (), s32[]{:S(2)}) async-start(), calls=%async_computation.2 | async-start | bytes 524288 | tf_op jit(solution)/shard_map/psum | solution.py:75
Sparse Core Ops, SparseCore 0:
  245.2 101.6 all-reduce.3
  350.4 97.4 all-reduce.5
  451.1 406.9 all-reduce.7
